TPU v7x, 32 devices: a whole 2x2x4 slice. The times are simulated.
32 devices in a mesh: row: 4 (over y, x), col: 8 (over z, core).
Axes of the slice: x: 2, y: 2, z: 4, core: 2. Of those that a mesh axis runs over, the one named last changes fastest.
Arguments:
- block_input: float32 [2, 8192, 640], P(None, ('row', 'col')), may hold values from -6 to 6
- output_grad: float32 [2, 8192, 640], P(None, ('row', 'col')), may hold values from -6 to 6
- sequence_ids: int32 [2, 8192], P(None, ('row', 'col')), may hold values from 0 to 7, as said below
- attn_weights: float32 [640, 2560], P(None, ('row', 'col')), may hold values from -0.29646353 to 0.29646353
- attn_momentum: float32 [640, 2560], P(None, ('row', 'col')), may hold values from -422.4 to 422.4
- attn_average: float32 [640, 2560], P(None, ('row', 'col')), may hold values from -0.29646353 to 0.29646353
- norm_params: float32 [2560], P(('row', 'col')), may hold values from -0.6 to 1.3
- norm_momentum: float32 [2560], P(('row', 'col')), may hold values from -806.4 to 806.4
- norm_average: float32 [2560], P(('row', 'col')), may hold values from -0.6 to 1.3
- ffn_weights: float32 [2, 640, 5120], P(None, 'row', 'col'), may hold values from -0.118585412 to 0.118585412
- ffn_momentum: float32 [2, 640, 5120], P(None, 'row', 'col'), may hold values from -249.6 to 249.6
- ffn_average: float32 [2, 640, 5120], P(None, 'row', 'col'), may hold values from -0.118585412 to 0.118585412
Outputs:
- block_output: float32 [2, 8192, 640], P(None, ('row', 'col'))
- input_grad: float32 [2, 8192, 640], P(None, ('row', 'col'))
- attn_grad: float32 [640, 2560], P(None, ('row', 'col'))
- attn_momentum_new: float32 [640, 2560], P(None, ('row', 'col'))
- attn_weights_new: float32 [640, 2560], P(None, ('row', 'col'))
- attn_average_new: float32 [640, 2560], P(None, ('row', 'col'))
- attn_copy: bfloat16 [640, 2560], P(None, ('row', 'col'))
- norm_grad: float32 [2560], P(('row', 'col'))
- norm_momentum_new: float32 [2560], P(('row', 'col'))
- norm_params_new: float32 [2560], P(('row', 'col'))
- norm_average_new: float32 [2560], P(('row', 'col'))
- norm_copy: bfloat16 [2560], P(('row', 'col'))
- ffn_grad: float32 [2, 640, 5120], P(None, 'row', 'col')
- ffn_momentum_new: float32 [2, 640, 5120], P(None, 'row', 'col')
- ffn_weights_new: float32 [2, 640, 5120], P(None, 'row', 'col')
- ffn_average_new: float32 [2, 640, 5120], P(None, 'row', 'col')
- ffn_copy: bfloat16 [2, 640, 5120], P(None, 'row', 'col')
Inputs may be any that keep to these rules, and one draw needn't show every extreme that they name: `sequence_ids`: within each aligned block of 256 tokens the numbers start at 0, never fall and step by one; a sequence (a run of equal numbers) holds 20 to 256 tokens; in each micro-batch one block holds a single sequence and another holds 8 sequences.
All inputs are finite; a program needn't handle non-finite values.
Results may differ from a plain program's by a relative error of at most 0.014.
The roundings to bfloat16 on the way count: a program that leaves them out, or rounds other values in their place, can miss the bound.
Values may be sent and summed in bfloat16 or wider, within the bound.
A program may use at most 128 MiB of HBM per device.

v0:
```python
import math
import jax
import jax.numpy as jnp
from jax import lax
from jax.sharding import PartitionSpec as P

D = 640
H = 20
HD = 32
MB = 2
EPSILON = 1e-05
MOMENT_DECAY = 0.9
AVERAGE_DECAY = 0.85
RATE_SCALE = 0.06
MASKED = -1e30


def layer_norm(values, gain, shift):
    center = values - jnp.mean(values, axis=-1, keepdims=True)
    spread = jnp.mean(center * center, axis=-1, keepdims=True)
    return center * lax.rsqrt(spread + EPSILON) * gain + shift


def gelu_exact(values):
    return jax.nn.gelu(values, approximate=False)


def matmul(left_side, right_side):
    return jnp.dot(left_side, right_side, preferred_element_type=jnp.float32)


def contract_rows(left_side, right_side):
    return lax.dot_general(
        left_side, right_side, (((0,), (0,)), ((), ())), preferred_element_type=jnp.float32
    )


def contract_cols(left_side, right_side):
    return lax.dot_general(
        left_side, right_side, (((1,), (1,)), ((), ())), preferred_element_type=jnp.float32
    )


def head_slices(qkv_low, first_col, head_group):
    length = qkv_low.shape[0]
    group_width = head_group * HD
    queries = lax.dynamic_slice_in_dim(qkv_low, first_col, group_width, 1).reshape(
        length, head_group, HD
    )
    keys_part = lax.dynamic_slice_in_dim(qkv_low, D + first_col, group_width, 1).reshape(
        length, head_group, HD
    )
    values = lax.dynamic_slice_in_dim(qkv_low, 2 * D + first_col, group_width, 1).reshape(
        length, head_group, HD
    )
    return (queries, keys_part, values)


def masked_scores(queries, keys_part, same_seq):
    scores = jnp.einsum(
        "qhe,khe->hqk", queries, keys_part, preferred_element_type=jnp.float32
    ) * HD ** (-0.5)
    return jnp.where(same_seq[None], scores, MASKED)


def attend_forward(qkv_low, same_seq):
    length = qkv_low.shape[0]
    head_group = math.gcd(H, 4)
    group_width = head_group * HD

    def one_group(group_index, state_all):
        mixed_all, maxima, totals = state_all
        first_col = group_index * group_width
        queries, keys_part, values = head_slices(qkv_low, first_col, head_group)
        scores = masked_scores(queries, keys_part, same_seq)
        row_max = jnp.max(scores, axis=-1, keepdims=True)
        exponent = jnp.exp(scores - row_max)
        row_total = jnp.sum(exponent, axis=-1, keepdims=True)
        attn_probs = (exponent / row_total).astype(jnp.bfloat16)
        mixed_rows = jnp.einsum(
            "hqk,khe->qhe", attn_probs, values, preferred_element_type=jnp.float32
        )
        mixed_all = lax.dynamic_update_slice_in_dim(
            mixed_all, mixed_rows.reshape(length, group_width), first_col, 1
        )
        maxima = lax.dynamic_update_slice_in_dim(
            maxima, row_max[:, :, 0], group_index * head_group, 0
        )
        totals = lax.dynamic_update_slice_in_dim(
            totals, row_total[:, :, 0], group_index * head_group, 0
        )
        return (mixed_all, maxima, totals)

    initial = (
        jnp.zeros((length, D), jnp.float32),
        jnp.zeros((H, length), jnp.float32),
        jnp.zeros((H, length), jnp.float32),
    )
    return lax.fori_loop(0, H // head_group, one_group, initial)


def attend_backward(qkv_low, same_seq, maxima, totals, grad_mixed):
    length = qkv_low.shape[0]
    head_group = math.gcd(H, 4)
    group_width = head_group * HD

    def one_group(group_index, grad_qkv):
        first_col = group_index * group_width
        queries, keys_part, values = head_slices(qkv_low, first_col, head_group)
        grad_part = lax.dynamic_slice_in_dim(grad_mixed, first_col, group_width, 1).reshape(
            length, head_group, HD
        )
        scores = masked_scores(queries, keys_part, same_seq)
        row_max = lax.dynamic_slice_in_dim(maxima, group_index * head_group, head_group, 0)[
            :, :, None
        ]
        row_total = lax.dynamic_slice_in_dim(totals, group_index * head_group, head_group, 0)[
            :, :, None
        ]
        attn_probs = jnp.exp(scores - row_max) / row_total
        grad_probs = jnp.einsum(
            "qhe,khe->hqk", grad_part, values, preferred_element_type=jnp.float32
        )
        grad_values = jnp.einsum(
            "hqk,qhe->khe",
            attn_probs.astype(jnp.bfloat16),
            grad_part,
            preferred_element_type=jnp.float32,
        )
        grad_scores = attn_probs * (
            grad_probs - jnp.sum(grad_probs * attn_probs, axis=-1, keepdims=True)
        )
        grad_scores = grad_scores.astype(jnp.bfloat16)
        grad_queries = jnp.einsum(
            "hqk,khe->qhe", grad_scores, keys_part, preferred_element_type=jnp.float32
        ) * HD ** (-0.5)
        grad_keys = jnp.einsum(
            "hqk,qhe->khe", grad_scores, queries, preferred_element_type=jnp.float32
        ) * HD ** (-0.5)
        for offset, grad_piece in ((0, grad_queries), (D, grad_keys), (2 * D, grad_values)):
            grad_qkv = lax.dynamic_update_slice_in_dim(
                grad_qkv, grad_piece.reshape(length, group_width), offset + first_col, 1
            )
        return grad_qkv

    return lax.fori_loop(0, H // head_group, one_group, jnp.zeros((length, 3 * D), jnp.float32))


def sgd_update(weights_old, moment, average, grad_sum, step_rate):
    moment_new = MOMENT_DECAY * moment + grad_sum
    weights_new = weights_old - step_rate * (grad_sum + MOMENT_DECAY * moment_new)
    average_new = AVERAGE_DECAY * average + (1.0 - AVERAGE_DECAY) * weights_new
    return (moment_new, weights_new, average_new, weights_new.astype(jnp.bfloat16))


def local(
    block_input,
    output_grad,
    sequence_ids,
    attn_weights,
    attn_momentum,
    attn_average,
    norm_params,
    norm_momentum,
    norm_average,
    ffn_weights,
    ffn_momentum,
    ffn_average,
):
    attn_full, norm_full = (
        lax.all_gather(attn_weights.astype(jnp.bfloat16), ("row", "col"), axis=1, tiled=True),
        lax.all_gather(norm_params.astype(jnp.bfloat16), ("row", "col"), axis=0, tiled=True),
    )
    norm_values = norm_full.astype(jnp.float32)
    gain_one = norm_values[:D]
    shift_one = norm_values[D : 2 * D]
    gain_two = norm_values[2 * D : 3 * D]
    shift_two = norm_values[3 * D :]
    qkv_weights = attn_full[:, : 3 * D]
    out_weights = attn_full[:, 3 * D :]
    ffn_rows = lax.all_gather(ffn_weights.astype(jnp.bfloat16), "row", axis=1, tiled=True)
    col_width = ffn_weights.shape[2]
    length = block_input.shape[1]
    attn_acc = jnp.zeros((D, 4 * D), jnp.float32)
    norm_acc = jnp.zeros((4 * D,), jnp.float32)
    ffn_acc = jnp.zeros((2, D, col_width), jnp.float32)
    outputs_all = []
    grads_all = []
    for micro_step in range(MB):
        inputs = block_input[micro_step]
        ids_row = sequence_ids[micro_step]
        same_seq = ids_row[:, None] == ids_row[None, :]
        normed, pull_one = jax.vjp(layer_norm, inputs, gain_one, shift_one)
        normed_low = normed.astype(jnp.bfloat16)
        qkv_low = matmul(normed_low, qkv_weights).astype(jnp.bfloat16)
        mixed_all, maxima, totals = attend_forward(qkv_low, same_seq)
        mixed_low = mixed_all.astype(jnp.bfloat16)
        hidden_in = inputs + matmul(mixed_low, out_weights)
        normed_two, pull_two = jax.vjp(layer_norm, hidden_in, gain_two, shift_two)
        normed_two_low = normed_two.astype(jnp.bfloat16)
        grad_out = output_grad[micro_step]
        grad_out_low = grad_out.astype(jnp.bfloat16)
        normed_all = lax.all_gather(normed_two_low, "col", axis=0, tiled=True)
        up_proj = matmul(normed_all, ffn_rows[0])
        activation, pull_gelu = jax.vjp(gelu_exact, up_proj)
        activ_low = activation.astype(jnp.bfloat16)
        ffn_out = lax.psum_scatter(
            contract_cols(activ_low, ffn_rows[1]).astype(jnp.bfloat16),
            "col",
            scatter_dimension=0,
            tiled=True,
        ).astype(jnp.float32)
        grad_all = lax.all_gather(grad_out_low, "col", axis=0, tiled=True)
        grad_act = matmul(grad_all, ffn_rows[1])
        grad_up = pull_gelu(grad_act)[0].astype(jnp.bfloat16)
        grad_normed_two = lax.psum_scatter(
            contract_cols(grad_up, ffn_rows[0]).astype(jnp.bfloat16),
            "col",
            scatter_dimension=0,
            tiled=True,
        ).astype(jnp.float32)
        ffn_acc = ffn_acc + jnp.stack(
            [contract_rows(normed_all, grad_up), contract_rows(grad_all, activ_low)]
        )
        outputs_all.append(hidden_in + ffn_out)
        grad_ln_two, gain_two_grad, shift_two_grad = pull_two(grad_normed_two)
        grad_hidden = grad_out + grad_ln_two
        grad_branch_low = grad_hidden.astype(jnp.bfloat16)
        out_proj_grad = contract_rows(mixed_low, grad_branch_low)
        grad_mixed_low = contract_cols(grad_branch_low, out_weights).astype(jnp.bfloat16)
        grad_qkv_low = attend_backward(qkv_low, same_seq, maxima, totals, grad_mixed_low).astype(
            jnp.bfloat16
        )
        qkv_grad = contract_rows(normed_low, grad_qkv_low)
        grad_normed = contract_cols(grad_qkv_low, qkv_weights)
        grad_ln_one, gain_one_grad, shift_one_grad = pull_one(grad_normed)
        grads_all.append(grad_hidden + grad_ln_one)
        attn_acc = attn_acc + jnp.concatenate([qkv_grad, out_proj_grad], axis=1)
        norm_acc = norm_acc + jnp.concatenate(
            [gain_one_grad, shift_one_grad, gain_two_grad, shift_two_grad]
        )
    ffn_grad = lax.psum_scatter(
        ffn_acc.astype(jnp.bfloat16), "row", scatter_dimension=1, tiled=True
    ).astype(jnp.float32)
    attn_grad, norm_grad = (
        lax.psum_scatter(attn_acc, ("row", "col"), scatter_dimension=1, tiled=True),
        lax.psum_scatter(norm_acc, ("row", "col"), scatter_dimension=0, tiled=True),
    )
    total_tokens = MB * length * lax.axis_size("row") * lax.axis_size("col")
    step_rate = RATE_SCALE * total_tokens ** (-0.5)
    attn_moment_new, attn_new, attn_avg_new, attn_copy = sgd_update(
        attn_weights, attn_momentum, attn_average, attn_grad, step_rate
    )
    norm_moment_new, norm_new, norm_avg_new, norm_copy = sgd_update(
        norm_params, norm_momentum, norm_average, norm_grad, step_rate
    )
    ffn_moment_new, ffn_new, ffn_avg_new, ffn_copy = sgd_update(
        ffn_weights, ffn_momentum, ffn_average, ffn_grad, step_rate
    )
    return (
        jnp.stack(outputs_all),
        jnp.stack(grads_all),
        attn_grad,
        attn_moment_new,
        attn_new,
        attn_avg_new,
        attn_copy,
        norm_grad,
        norm_moment_new,
        norm_new,
        norm_avg_new,
        norm_copy,
        ffn_grad,
        ffn_moment_new,
        ffn_new,
        ffn_avg_new,
        ffn_copy,
    )


def solution(mesh):
    return jax.shard_map(
        local,
        mesh=mesh,
        in_specs=(
            P(None, ("row", "col"), None),
            P(None, ("row", "col"), None),
            P(None, ("row", "col")),
            P(None, ("row", "col")),
            P(None, ("row", "col")),
            P(None, ("row", "col")),
            P(("row", "col")),
            P(("row", "col")),
            P(("row", "col")),
            P(None, "row", "col"),
            P(None, "row", "col"),
            P(None, "row", "col"),
        ),
        out_specs=(
            P(None, ("row", "col"), None),
            P(None, ("row", "col"), None),
            P(None, ("row", "col")),
            P(None, ("row", "col")),
            P(None, ("row", "col")),
            P(None, ("row", "col")),
            P(None, ("row", "col")),
            P(("row", "col")),
            P(("row", "col")),
            P(("row", "col")),
            P(("row", "col")),
            P(("row", "col")),
            P(None, "row", "col"),
            P(None, "row", "col"),
            P(None, "row", "col"),
            P(None, "row", "col"),
            P(None, "row", "col"),
        ),
        check_vma=False,
    )
```

profile of v0, /device:TPU:0, one launch (start us, length us, event | category | flops | bytes accessed | tf_op | source)
XLA Modules:
  0.0 634.6 jit_solution(1245583940344998893)
XLA Ops:
  7.2 1.6 convert_element_type.174
  8.9 1.9 convert_element_type.178
  12.3 1.4 slice_reduce_fusion.1
  13.8 1.6 multiply_reduce_fusion.9
  16.0 42.1 %all-reduce = bf16[2560]{0:T(1024)(128)(2,1)S(1)} all-reduce(bf16[2560]{0:T(1024)(128)(2,1)S(1)} %dynamic-update-slice), channel_id=1, replica_groups=mesh['row'=4,'col'=8] {'row','col'}, use_global_device_ids=true, to_apply=%add | all-reduce | flops 2560 | bytes 10240
  58.1 15.5 %all-gather.7.cloned.1.call-done = bf16[640,2560]{0,1:T(8,128)(2,1)} async-done(((bf16[640,80]{0,1:T(8,128)(2,1)}), bf16[640,2560]{0,1:T(8,128)(2,1)}) %all-gather.7.cloned.1.call-update) | async-done | bytes 3276816 | tf_op jit(solution)/shard_map/all_gather | solution.py:171
  73.6 3.0 convolution_convert_fusion.4
  77.3 5.3 while.73
  85.1 4.0 convolution_convert_fusion.5
  89.2 1.6 copy.63
  91.5 8.2 %while.72 = (s32[]{:T(128)}, bf16[256,640]{0,1:T(8,128)(2,1)}, f32[20,256]{1,0:T(8,128)S(1)}, f32[20,256]{1,0:T(8,128)S(1)}, bf16[256,1920]{0,1:T(8,128)(2,1)S(1...) while((s32[]{:T(128)}, bf16[256,640]{0,1:T(8,128)(2,1)}, ...), condition=%wide.region_5.6_spmd.clone, body=%wide.region_2.5_spmd.clone.sunk | while | flops 35715084 | bytes 4101494 | solution.py:99
  99.7 2.2 fusion.95
  102.1 1.8 fusion.94
  104.2 1.1 add_convert_fusion.4
  105.4 2.2 bitcast_convert_fusion.1
  109.0 33.7 %all-gather.9.cloned.1.call-done = bf16[2048,640]{1,0:T(8,128)(2,1)} async-done(((bf16[256,640]{1,0:T(8,128)(2,1)}), bf16[2048,640]{1,0:T(8,128)(2,1)}) %all-gather.9.cloned.1.call-update) | async-done | bytes 2621456 | tf_op jit(solution)/shard_map/all_gather | solution.py:203
  142.7 16.6 %multiply_convert_fusion.3 = (bf16[2048,640]{1,0:T(8,128)(2,1)}, f32[2048,640]{1,0:T(8,128)}, f32[2048,640]{1,0:T(8,128)}) fusion(bf16[2048,640]{1,0:T(8,128)(2,1)} %all-gather.9.cloned.1.call-done, bf16[2,640,640]{2,1,0:T(8,128)(2,1)} %all-gather.11.cloned.1.call-done), kind=kOutput, calls=%fused_computation.92 | convolution fusion | flops 1762918400 | bytes 16547840 | tf_op jit(solution)/shard_map/dot_general | solution.py:29
  159.3 17.8 %all-gather.15.cloned.1.call-done = bf16[2048,640]{1,0:T(8,128)(2,1)} async-done(((bf16[256,640]{1,0:T(8,128)(2,1)}), bf16[2048,640]{1,0:T(8,128)(2,1)}) %all-gather.15.cloned.1.call-update) | async-done | bytes 2621456 | tf_op jit(solution)/shard_map/all_gather | solution.py:213
  177.1 8.6 %add_convert_fusion.1 = bf16[2048,640]{1,0:T(8,128)(2,1)S(1)} fusion(f32[2048,640]{1,0:T(8,128)} %get-tuple-element.929, f32[2048,640]{1,0:T(8,128)} %get-tuple-element.981, bf16[2048,640]{1,0:T(8,128)(2,1)} %all-gather.15.cloned.1.call-done, bf16[2,640,640]{2,1,0:T(8,128)(2,1)} %all-gather.11.cloned.1.call-done), kind=kOutput, calls=%fused_computation.78 | convolution fusion | flops 1696071680 | bytes 16547840 | tf_op jit(solution)/shard_map/dot_general | solution.py:29
  185.7 1.5 copy-done.16
  187.1 3.8 convolution_convert_fusion.1
  191.2 20.9 %all-gather.13.cloned.1.call-done = bf16[2048,640]{1,0:T(8,128)(2,1)} async-done(((bf16[256,640]{1,0:T(8,128)(2,1)}), bf16[2048,640]{1,0:T(8,128)(2,1)}) %all-gather.13.cloned.1.call-update) | async-done | bytes 2621456 | tf_op jit(solution)/shard_map/all_gather | solution.py:203
  212.0 16.5 %multiply_convert_fusion.2 = (bf16[2048,640]{1,0:T(8,128)(2,1)}, f32[2048,640]{1,0:T(8,128)}, f32[2048,640]{1,0:T(8,128)}) fusion(bf16[2048,640]{1,0:T(8,128)(2,1)} %all-gather.13.cloned.1.call-done, bf16[2,640,640]{2,1,0:T(8,128)(2,1)} %all-gather.11.cloned.1.call-done), kind=kOutput, calls=%fused_computation.79 | convolution fusion | flops 1762918400 | bytes 16547840 | tf_op jit(solution)/shard_map/dot_general | solution.py:29
  228.6 17.9 %all-gather.17.cloned.1.call-done = bf16[2048,640]{1,0:T(8,128)(2,1)} async-done(((bf16[256,640]{1,0:T(8,128)(2,1)}), bf16[2048,640]{1,0:T(8,128)(2,1)}) %all-gather.17.cloned.1.call-update) | async-done | bytes 2621456 | tf_op jit(solution)/shard_map/all_gather | solution.py:213
  246.4 8.6 %add_convert_fusion = bf16[2048,640]{1,0:T(8,128)(2,1)S(1)} fusion(f32[2048,640]{1,0:T(8,128)} %get-tuple-element.931, f32[2048,640]{1,0:T(8,128)} %get-tuple-element.982, bf16[2048,640]{1,0:T(8,128)(2,1)} %all-gather.17.cloned.1.call-done, bf16[2,640,640]{2,1,0:T(8,128)(2,1)} %all-gather.11.cloned.1.call-done), kind=kOutput, calls=%fused_computation.77 | convolution fusion | flops 1696071680 | bytes 16547840 | tf_op jit(solution)/shard_map/dot_general | solution.py:29
  255.0 1.5 copy-done.18
  256.6 3.7 convolution_convert_fusion
  260.4 6.0 convolution_convert_fusion.2
  266.8 5.9 convolution_convert_fusion.3
  272.9 5.0 convolution_bitcast_fusion
  277.9 2.3 convolution_bitcast_fusion.1
  280.5 2.4 convolution_bitcast_fusion.2
  283.1 2.3 convolution_bitcast_fusion.3
  285.4 1.5 fusion.38
  287.1 1.2 fusion.50
  288.3 35.8 %reduce-scatter.15.cloned.1.call-done = bf16[256,640]{1,0:T(8,128)(2,1)} async-done(((bf16[2048,640]{1,0:T(8,128)(2,1)}), bf16[256,640]{1,0:T(8,128)(2,1)}) %reduce-scatter.15.cloned.1.call-update) | async-done | bytes 327696 | tf_op jit(solution)/shard_map/reduce_scatter | solution.py:216
  324.1 1.6 fusion.51
  325.7 1.4 fusion.52
  327.1 36.2 %reduce-scatter.11.cloned.1.call-done = bf16[256,640]{1,0:T(8,128)(2,1)} async-done(((bf16[2048,640]{1,0:T(8,128)(2,1)}), bf16[256,640]{1,0:T(8,128)(2,1)}) %reduce-scatter.11.cloned.1.call-update) | async-done | bytes 327696 | tf_op jit(solution)/shard_map/reduce_scatter | solution.py:207
  363.3 38.9 %reduce-scatter.9.cloned.1.call-done = bf16[256,640]{1,0:T(8,128)(2,1)} async-done(((bf16[2048,640]{1,0:T(8,128)(2,1)}), bf16[256,640]{1,0:T(8,128)(2,1)}) %reduce-scatter.9.cloned.1.call-update) | async-done | bytes 327696 | tf_op jit(solution)/shard_map/reduce_scatter | solution.py:207
  402.1 2.8 bitcast_add_fusion.1
  405.7 1.6 convolution_convert_fusion.7
  407.4 15.2 %while.74 = (s32[]{:T(128)}, bf16[256,1920]{0,1:T(8,128)(2,1)S(1)}, bf16[256,1920]{0,1:T(8,128)(2,1)}, f32[20,256]{1,0:T(8,128)S(1)}, f32[20,256]{1,0:T(8,128)S(...) while((s32[]{:T(128)}, bf16[256,1920]{0,1:T(8,128)(2,1)S(1)}, ...), condition=%wide.region_23.24_spmd.clone, body=%wide.region_21.0_spmd.clone.sunk | while | flops 86703120 | bytes 9733514 | solution.py:146
  413.8 0.9 constant_dynamic-slice_fusion.28
  416.9 0.9 constant_dynamic-slice_fusion.28
  422.6 2.7 convolution_convert_fusion.6
  425.3 1.0 broadcast.368.clone
  426.4 31.9 %while.75 = (s32[]{:T(128)}, bf16[256,1920]{0,1:T(8,128)(2,1)}, bf16[256,1920]{0,1:T(8,128)(2,1)}, f32[20,256]{1,0:T(8,128)}, f32[20,256]{1,0:T(8,128)}, /*index...) while((s32[]{:T(128)}, bf16[256,1920]{0,1:T(8,128)(2,1)}, ...), condition=%wide.region_31.32_spmd.clone, body=%wide.region_29.0_spmd.clone.sunk | while | flops 86703120 | bytes 9733514 | solution.py:146
  458.7 1.4 fusion.70
  460.2 2.3 fusion.61
  462.6 1.0 fusion.64
  463.6 3.2 maximum_add_fusion
  466.9 8.2 %copy.93 = f32[640,2560]{0,1:T(8,128)} copy(f32[640,2560]{1,0:T(8,128)} %maximum_add_fusion) | data formatting | bytes 13107200
  478.7 3.2 fusion.83
  481.9 2.5 multiply_add_fusion
  484.4 2.3 fusion.39
  486.7 2.1 multiply_reduce_fusion.3
  488.8 39.0 %all-reduce.1 = f32[2560]{0:T(1024)S(1)} all-reduce(f32[2560]{0:T(1024)S(1)} %maximum_add_fusion.2), channel_id=7, replica_groups=mesh['row'=4,'col'=8] {'row','col'}, use_global_device_ids=true, to_apply=%region_43.44.clone | all-reduce | flops 2560 | bytes 20480
  527.8 2.2 pad_maximum_fusion
  530.1 1.8 fusion.86
  532.3 1.1 pad_maximum_fusion.1
  534.5 87.4 %reduce-scatter.19.cloned.1.call-done = f32[80,640]{1,0:T(8,128)} async-done(((f32[2560,640]{1,0:T(8,128)}), f32[80,640]{1,0:T(8,128)}) %reduce-scatter.19.cloned.1.call-update) | async-done | bytes 204816
  622.0 1.1 copy.94
  624.0 1.0 multiply_add_fusion.2
  (387 shorter events, 76.7 us)
Async XLA Ops:
  7.2 66.4 %all-gather.7.cloned.1.call-start = ((), (), s32[]{:S(2)}) async-start(), calls=%async_computation.6 | async-start | bytes 3379200 | tf_op jit(solution)/shard_map/all_gather | solution.py:171
  8.8 100.2 %all-gather.11.cloned.1.call-start = ((), (), s32[]{:S(2)}) async-start(), calls=%async_computation.8 | async-start | bytes 2048000 | tf_op jit(solution)/shard_map/all_gather | solution.py:181
  10.9 131.8 %all-gather.9.cloned.1.call-start = ((), (), s32[]{:S(2)}) async-start(), calls=%async_computation.7 | async-start | bytes 2949120 | tf_op jit(solution)/shard_map/all_gather | solution.py:203
  13.8 63.5 %copy-start.35 = (f32[256]{0:T(256)}, f32[256]{0:T(256)S(1)}, u32[]{:S(2)}) copy-start(f32[256]{0:T(256)S(1)} %get-tuple-element.984) | copy-start | bytes 3076
  13.8 68.8 %copy-start.37 = (f32[256]{0:T(256)}, f32[256]{0:T(256)S(1)}, u32[]{:S(2)}) copy-start(f32[256]{0:T(256)S(1)} %get-tuple-element.985) | copy-start | bytes 3076
  15.4 67.2 %copy-start.39 = (f32[256]{0:T(256)}, f32[256]{0:T(256)S(1)}, u32[]{:S(2)}) copy-start(f32[256]{0:T(256)S(1)} %fusion.77) | copy-start | bytes 3076
  15.4 61.8 %copy-start.41 = (f32[256]{0:T(256)}, f32[256]{0:T(256)S(1)}, u32[]{:S(2)}) copy-start(f32[256]{0:T(256)S(1)} %fusion.79) | copy-start | bytes 3076
  58.0 24.6 %copy-start.27 = (f32[640]{0:T(1024)}, f32[640]{0:T(1024)S(1)}, u32[]{:S(2)}) copy-start(f32[640]{0:T(1024)S(1)} %get-tuple-element.973) | copy-start | bytes 7684
  58.0 24.6 %copy-start.29 = (f32[640]{0:T(1024)}, f32[640]{0:T(1024)S(1)}, u32[]{:S(2)}) copy-start(f32[640]{0:T(1024)S(1)} %get-tuple-element.974) | copy-start | bytes 7684
  77.3 7.9 %copy-start = (f32[2,256,640]{2,1,0:T(8,128)S(1)}, f32[2,256,640]{2,1,0:T(8,128)}, u32[]{:S(2)}) copy-start(f32[2,256,640]{2,1,0:T(8,128)} %param.20) | copy-start | bytes 3932164
  82.6 0.7 copy-start.11
  83.9 0.6 copy-start.33
  84.5 0.6 copy-start.34
  85.1 6.4 %copy-start.4 = (bf16[256,1920]{0,1:T(8,128)(2,1)}, bf16[256,1920]{0,1:T(8,128)(2,1)S(1)}, u32[]{:S(2)}) copy-start(bf16[256,1920]{0,1:T(8,128)(2,1)S(1)} %get-tuple-element.1414) | copy-start | bytes 2949124
  99.7 2.4 copy-start.5
  105.4 71.7 %all-gather.15.cloned.1.call-start = ((), (), s32[]{:S(2)}) async-start(), calls=%async_computation.12 | async-start | bytes 2949120 | tf_op jit(solution)/shard_map/all_gather | solution.py:213
  107.6 104.4 %all-gather.13.cloned.1.call-start = ((), (), s32[]{:S(2)}) async-start(), calls=%async_computation.10 | async-start | bytes 2949120 | tf_op jit(solution)/shard_map/all_gather | solution.py:203
  108.2 138.2 %all-gather.17.cloned.1.call-start = ((), (), s32[]{:S(2)}) async-start(), calls=%async_computation.14 | async-start | bytes 2949120 | tf_op jit(solution)/shard_map/all_gather | solution.py:213
  108.8 178.3 %reduce-scatter.13.cloned.1.call-start = ((), (), s32[]{:S(2)}) async-start(), calls=%async_computation.13 | async-start | bytes 2949120 | tf_op jit(solution)/shard_map/reduce_scatter | solution.py:216
  177.1 10.1 %copy-start.51 = (bf16[2,640,640]{2,1,0:T(8,128)(2,1)S(1)}, bf16[2,640,640]{2,1,0:T(8,128)(2,1)}, u32[]{:S(2)}) copy-start(bf16[2,640,640]{2,1,0:T(8,128)(2,1)} %all-gather.11.cloned.1.call-done) | copy-start | bytes 4915204
  185.6 1.5 copy-start.16
  190.9 133.2 %reduce-scatter.15.cloned.1.call-start = ((), (), s32[]{:S(2)}) async-start(), calls=%async_computation.15 | async-start | bytes 2949120 | tf_op jit(solution)/shard_map/reduce_scatter | solution.py:216
  246.4 10.1 %copy-start.52 = (bf16[2,640,640]{2,1,0:T(8,128)(2,1)S(1)}, bf16[2,640,640]{2,1,0:T(8,128)(2,1)}, u32[]{:S(2)}) copy-start(bf16[2,640,640]{2,1,0:T(8,128)(2,1)} %all-gather.11.cloned.1.call-done) | copy-start | bytes 4915204
  255.0 1.6 copy-start.18
  260.3 102.9 %reduce-scatter.11.cloned.1.call-start = ((), (), s32[]{:S(2)}) async-start(), calls=%async_computation.11 | async-start | bytes 2949120 | tf_op jit(solution)/shard_map/reduce_scatter | solution.py:207
  266.4 135.7 %reduce-scatter.9.cloned.1.call-start = ((), (), s32[]{:S(2)}) async-start(), calls=%async_computation.9 | async-start | bytes 2949120 | tf_op jit(solution)/shard_map/reduce_scatter | solution.py:207
  272.8 205.9 %reduce-scatter.17.cloned.1.call-start = ((), (), s32[]{:S(2)}) async-start(), calls=%async_computation.16 | async-start | bytes 2048000 | tf_op jit(solution)/shard_map/reduce_scatter | solution.py:242
  272.9 5.0 copy-start.15
  272.9 5.0 copy-start.19
  277.9 2.3 copy-start.50
  277.9 2.6 copy-start.54
  280.5 2.4 copy-start.14
  280.5 2.6 copy-start.17
  285.4 116.8 %copy-start.13 = (f32[2,256,640]{2,1,0:T(8,128)S(1)}, f32[2,256,640]{2,1,0:T(8,128)}, u32[]{:S(2)}) copy-start(f32[2,256,640]{2,1,0:T(8,128)} %param.21) | copy-start | bytes 3932164
  286.9 335.1 %reduce-scatter.19.cloned.1.call-start = ((), (), s32[]{:S(2)}) async-start(), calls=%async_computation.17 | async-start | bytes 6758400
  404.9 0.8 copy-start.2
  407.4 18.9 %copy-start.26 = (s32[256]{0:T(256)S(1)}, s32[256]{0:T(256)}, u32[]{:S(2)}) copy-start(s32[256]{0:T(256)} %copy-done.25) | copy-start | bytes 3076
  422.6 3.7 copy-start.6
  426.3 31.9 %copy-start.12 = (bf16[256,640]{0,1:T(8,128)(2,1)S(1)}, bf16[256,640]{0,1:T(8,128)(2,1)}, u32[]{:S(2)}) copy-start(bf16[256,640]{0,1:T(8,128)(2,1)} %copy-done.11) | copy-start | bytes 983044
  426.3 32.4 %copy-start.3 = (f32[256,640]{1,0:T(8,128)S(1)}, f32[256,640]{1,0:T(8,128)}, u32[]{:S(2)}) copy-start(f32[256,640]{1,0:T(8,128)} %copy-done.2) | copy-start | bytes 1966084
  458.3 1.9 copy-start.1
  458.3 1.9 copy-start.28
  458.3 1.9 copy-start.30
  458.3 1.9 copy-start.36
  458.3 1.9 copy-start.42
  460.1 2.4 copy-start.7
  460.2 2.4 copy-start.38
  460.2 2.4 copy-start.40
  475.0 0.9 copy-start.23
  475.0 1.8 copy-start.31
  475.0 2.7 copy-start.32
  478.7 5.7 copy-start.10
  481.9 6.9 %copy-start.9 = (f32[2,160,640]{2,1,0:T(8,128)}, f32[2,160,640]{2,1,0:T(8,128)S(1)}, u32[]{:S(2)}) copy-start(f32[2,160,640]{2,1,0:T(8,128)S(1)} %get-tuple-element.915) | copy-start | bytes 2457604
  481.9 4.8 copy-start.8
  484.4 43.4 %copy-start.20 = (f32[1,256,640]{2,1,0:T(8,128)S(1)}, f32[1,256,640]{2,1,0:T(8,128)}, u32[]{:S(2)}) copy-start(f32[1,256,640]{2,1,0:T(8,128)} %get-tuple-element.966) | copy-start | bytes 1966084
  486.7 2.1 copy-start.24
  486.7 43.3 %copy-start.46 = (f32[256]{0:T(256)S(1)}, f32[256]{0:T(256)}, u32[]{:S(2)}) copy-start(f32[256]{0:T(256)} %copy-done.45) | copy-start | bytes 3076
  486.7 43.3 %copy-start.44 = (f32[256]{0:T(256)S(1)}, f32[256]{0:T(256)}, u32[]{:S(2)}) copy-start(f32[256]{0:T(256)} %copy-done.43) | copy-start | bytes 3076
  530.1 3.3 copy-start.47
  530.1 3.3 copy-start.48
  530.1 3.9 copy-start.53
  531.9 91.1 %copy-start.21 = (f32[640,80]{1,0:T(8,128)S(1)}, f32[640,80]{1,0:T(8,128)}, u32[]{:S(2)}) copy-start(f32[640,80]{1,0:T(8,128)} %copy.72) | copy-start | bytes 614404
  531.9 91.1 %copy-start.22 = (f32[640,80]{1,0:T(8,128)S(1)}, f32[640,80]{1,0:T(8,128)}, u32[]{:S(2)}) copy-start(f32[640,80]{1,0:T(8,128)} %copy.71) | copy-start | bytes 614404
  534.0 93.5 %copy-start.49 = (f32[80]{0:T(128)}, f32[80]{0:T(128)S(1)}, u32[]{:S(2)}) copy-start(f32[80]{0:T(128)S(1)} %get-tuple-element.919) | copy-start | bytes 964
  (3 other events, 1.7 us)
Sparse Core Ops, SparseCore 0:
  11.4 62.0 all-gather.6
  76.0 30.5 all-gather.10
  108.8 33.8 all-gather.8
  144.2 32.8 all-gather.14
  179.1 32.8 all-gather.12
  213.5 32.8 all-gather.16
  248.7 36.4 reduce-scatter.12
  287.6 36.4 reduce-scatter.14
  326.4 36.8 reduce-scatter.10
  365.4 36.6 reduce-scatter.8
  405.1 30.4 reduce-scatter.16
  475.2 146.7 reduce-scatter.18
where the time goes:
time: 642 us; the launch traced here: 635 us
  waiting for transfers between devices  305 us (48%)
  matrix products  128 us (20%)
  blocking collectives  81.1 us (13%)
  local copies, waits for them, and re-layouts  62.4 us (10%)
  other arithmetic  39.3 us (6%)
  between operations  15.3 us (2%)
    unnamed x13, waiting for transfers between devices  88.6 us
    unnamed x2, blocking collectives  81.1 us
    reduce_scatter x2, waiting for transfers between devices, local(): lax.psum_scatter(contract_cols(activ_low, ffn_rows[1]).astype(jnp.bfloat1...  75 us
    dot_general x8, matrix products, matmul(): return jnp.dot(left_side, right_side, preferred_element_type=jnp.float32)  61.2 us
    all_gather x2, waiting for transfers between devices, local(): normed_all = lax.all_gather(normed_two_low, 'col', axis=0, tiled=True)  54.5 us
    reduce_scatter x2, waiting for transfers between devices, local(): lax.psum_scatter(contract_cols(grad_up, ffn_rows[0]).astype(jnp.bfloat16)...  35.8 us
    all_gather x2, waiting for transfers between devices, local(): grad_all = lax.all_gather(grad_out_low, 'col', axis=0, tiled=True)  35.7 us
    dot_general x8, matrix products, contract_cols(): lax.dot_general(left_side, right_side, (((1,), (1,)), ((), ())), preferre...  28 us
  transfers between devices with their start and end apart: 12, of which 9 were waited for; matrix products, arithmetic and copies ran while one was open for 34% of the time, Pallas kernels for 0%

commit v1 on v0

--- a/solution.py
+++ b/solution.py
@@ -200,7 +200,14 @@
         normed_two_low = normed_two.astype(jnp.bfloat16)
         grad_out = output_grad[micro_step]
         grad_out_low = grad_out.astype(jnp.bfloat16)
-        normed_all = lax.all_gather(normed_two_low, "col", axis=0, tiled=True)
+        ring = [normed_two_low]
+        for hop in range(7):
+            ring.append(lax.ppermute(ring[-1], "col", [(dev, (dev + 1) % 8) for dev in range(8)]))
+        normed_all = jnp.roll(
+            jnp.concatenate(ring[::-1], axis=0),
+            (lax.axis_index("col") + 1) * ring[0].shape[0],
+            axis=0,
+        )
         up_proj = matmul(normed_all, ffn_rows[0])
         activation, pull_gelu = jax.vjp(gelu_exact, up_proj)
         activ_low = activation.astype(jnp.bfloat16)

time: 642 us -> 619 us (0.964)
  waiting for transfers between devices: 305 us -> 259 us
  local copies, waits for them, and re-layouts: 62.4 us -> 83.8 us
    ppermute x0 -> x14, waiting for transfers between devices: none -> 75.9 us  [local(): lax.ppermute(ring[-1], 'col', [(dev, (dev + 1) % 8) for dev in range(8)])]
    all_gather x2 -> x0, waiting for transfers between devices: 54.5 us -> none  [local(): normed_all = lax.all_gather(normed_two_low, 'col', axis=0, tiled=True)]
    all_gather x2, waiting for transfers between devices: 35.7 us -> 0.01 us  [local(): grad_all = lax.all_gather(grad_out_low, 'col', axis=0, tiled=True)]
    reduce_scatter x2, waiting for transfers between devices: 35.8 us -> 6.46 us  [local(): lax.psum_scatter(contract_cols(grad_up, ffn_rows[0]).astype(jnp.bfloat16)...]
    unnamed x123 -> x187, local copies, waits for them, and re-layouts: 25.9 us -> 42.9 us
    unnamed x13 -> x11, waiting for transfers between devices: 88.6 us -> 88.3 us
  transfers between devices with their start and end apart: 12 -> 24, of which waited for: 9 -> 18; matrix products, arithmetic and copies ran while one was open for 34% -> 39% of each run, Pallas kernels for 0% -> 0%
where the time goes in v1:
time: 619 us; the launch traced here: 610 us
  waiting for transfers between devices  259 us (42%)
  matrix products  131 us (21%)
  local copies, waits for them, and re-layouts  83.8 us (14%)
  blocking collectives  81.2 us (13%)
  other arithmetic  35 us (6%)
  between operations  15.6 us (3%)
    unnamed x11, waiting for transfers between devices  88.3 us
    unnamed x2, blocking collectives  81.2 us
    ppermute x14, waiting for transfers between devices, local(): lax.ppermute(ring[-1], 'col', [(dev, (dev + 1) % 8) for dev in range(8)])  75.9 us
    reduce_scatter x2, waiting for transfers between devices, local(): lax.psum_scatter(contract_cols(activ_low, ffn_rows[1]).astype(jnp.bfloat1...  74.6 us
    dot_general x8, matrix products, matmul(): return jnp.dot(left_side, right_side, preferred_element_type=jnp.float32)  62 us
    unnamed x187, local copies, waits for them, and re-layouts  42.9 us
    dot_general x8, matrix products, contract_cols(): lax.dot_general(left_side, right_side, (((1,), (1,)), ((), ())), preferre...  28 us
    dot_general x8, matrix products, contract_rows(): lax.dot_general(left_side, right_side, (((0,), (0,)), ((), ())), preferre...  19.4 us
  transfers between devices with their start and end apart: 24, of which 18 were waited for; matrix products, arithmetic and copies ran while one was open for 39% of the time, Pallas kernels for 0%

profile of v1, /device:TPU:0, one launch (start us, length us, event | category | flops | bytes accessed | tf_op | source)
XLA Modules:
  0.0 610.1 jit_solution(15830985892892116673)
XLA Ops:
  7.2 1.7 convert_element_type.174
  9.0 1.9 convert_element_type.178
  11.0 2.2 bitcast_convert_fusion.1
  17.3 42.3 %all-reduce = bf16[2560]{0:T(1024)(128)(2,1)S(1)} all-reduce(bf16[2560]{0:T(1024)(128)(2,1)S(1)} %dynamic-update-slice), channel_id=1, replica_groups=mesh['row'=4,'col'=8] {'row','col'}, use_global_device_ids=true, to_apply=%add | all-reduce | flops 2560 | bytes 10240
  59.6 14.1 %all-gather.5.cloned.1.call-done = bf16[640,2560]{0,1:T(8,128)(2,1)} async-done(((bf16[640,80]{0,1:T(8,128)(2,1)}), bf16[640,2560]{0,1:T(8,128)(2,1)}) %all-gather.5.cloned.1.call-update) | async-done | bytes 3276816 | tf_op jit(solution)/shard_map/all_gather | solution.py:171
  73.7 2.7 convolution_convert_fusion.4
  77.2 5.3 while.73
  84.4 4.0 convolution_convert_fusion.5
  90.8 8.2 %while.72 = (s32[]{:T(128)}, bf16[256,640]{0,1:T(8,128)(2,1)}, f32[20,256]{1,0:T(8,128)S(1)}, f32[20,256]{1,0:T(8,128)S(1)}, bf16[256,1920]{0,1:T(8,128)(2,1)S(1...) while((s32[]{:T(128)}, bf16[256,640]{0,1:T(8,128)(2,1)}, ...), condition=%wide.region_5.6_spmd.clone, body=%wide.region_2.5_spmd.clone.sunk | while | flops 35715084 | bytes 4101494 | solution.py:99
  99.0 2.2 fusion.101
  101.5 1.8 fusion.100
  105.1 7.4 %collective-permute-done = bf16[256,640]{1,0:T(8,128)(2,1)S(1)} collective-permute-done((bf16[256,640]{1,0:T(8,128)(2,1)S(1)}, bf16[256,640]{1,0:T(8,128)(2,1)S(1)}, u32[]{:S(2)}, u32[]{:S(2)}) %collective-permute-start) | collective-permute-done | bytes 327712 | tf_op jit(solution)/shard_map/ppermute | solution.py:205
  112.5 3.5 collective-permute-done.7
  116.0 5.4 collective-permute-done.1
  121.4 10.5 %collective-permute-done.8 = bf16[256,640]{1,0:T(8,128)(2,1)S(1)} collective-permute-done((bf16[256,640]{1,0:T(8,128)(2,1)S(1)}, bf16[256,640]{1,0:T(8,128)(2,1)S(1)}, u32[]{:S(2)}, u32[]{:S(2)}) %collective-permute-start.8) | collective-permute-done | bytes 327712 | tf_op jit(solution)/shard_map/ppermute | solution.py:205
  131.9 10.5 %collective-permute-done.2 = bf16[256,640]{1,0:T(8,128)(2,1)S(1)} collective-permute-done((bf16[256,640]{1,0:T(8,128)(2,1)S(1)}, bf16[256,640]{1,0:T(8,128)(2,1)S(1)}, u32[]{:S(2)}, u32[]{:S(2)}) %collective-permute-start.2) | collective-permute-done | bytes 327712 | tf_op jit(solution)/shard_map/ppermute | solution.py:205
  142.4 10.0 %collective-permute-done.9 = bf16[256,640]{1,0:T(8,128)(2,1)S(1)} collective-permute-done((bf16[256,640]{1,0:T(8,128)(2,1)S(1)}, bf16[256,640]{1,0:T(8,128)(2,1)S(1)}, u32[]{:S(2)}, u32[]{:S(2)}) %collective-permute-start.9) | collective-permute-done | bytes 327712 | tf_op jit(solution)/shard_map/ppermute | solution.py:205
  152.4 3.5 collective-permute-done.3
  155.9 4.8 collective-permute-done.10
  160.7 3.5 collective-permute-done.4
  164.2 4.9 collective-permute-done.11
  169.1 3.5 collective-permute-done.5
  172.7 5.0 collective-permute-done.12
  177.9 3.3 collective-permute-done.6
  181.3 1.7 constant_dynamic-update-slice_fusion.19
  183.0 1.7 constant_dynamic-update-slice_fusion.18
  184.7 1.7 constant_dynamic-update-slice_fusion.17
  186.5 1.7 constant_dynamic-update-slice_fusion.16
  188.2 1.7 constant_dynamic-update-slice_fusion.15
  189.9 1.7 constant_dynamic-update-slice_fusion.14
  193.2 17.1 %multiply_convert_fusion.3 = (bf16[2048,640]{1,0:T(8,128)(2,1)}, f32[2048,640]{1,0:T(8,128)}, f32[2048,640]{1,0:T(8,128)}) fusion(bf16[2,640,640]{2,1,0:T(8,128)(2,1)} %all-gather.7.cloned.1.call-done, s32[]{:T(128)S(6)} %select_n.288, bf16[2048,640]{1,0:T(8,128)(2,1)} %constant_dynamic-update-slice_fusion.12), kind=kOutput, calls=%fused_computation.96 | convolution fusion | flops 1768161280 | bytes 16547844 | tf_op jit(solution)/shard_map/dot_general | solution.py:29
  210.3 8.6 %add_convert_fusion.1 = bf16[2048,640]{1,0:T(8,128)(2,1)S(1)} fusion(f32[2048,640]{1,0:T(8,128)} %get-tuple-element.930, f32[2048,640]{1,0:T(8,128)} %get-tuple-element.982, bf16[2048,640]{1,0:T(8,128)(2,1)} %all-gather.9.cloned.1.call-done, bf16[2,640,640]{2,1,0:T(8,128)(2,1)} %all-gather.7.cloned.1.call-done), kind=kOutput, calls=%fused_computation.82 | convolution fusion | flops 1696071680 | bytes 16547840 | tf_op jit(solution)/shard_map/dot_general | solution.py:29
  220.4 3.7 convolution_convert_fusion.1
  229.3 17.3 %multiply_convert_fusion.2 = (bf16[2048,640]{1,0:T(8,128)(2,1)}, f32[2048,640]{1,0:T(8,128)}, f32[2048,640]{1,0:T(8,128)}) fusion(bf16[2,640,640]{2,1,0:T(8,128)(2,1)} %all-gather.7.cloned.1.call-done, s32[]{:T(128)S(6)} %select_n.288, bf16[2048,640]{1,0:T(8,128)(2,1)S(1)} %constant_dynamic-update-slice_fusion.20), kind=kOutput, calls=%fused_computation.83 | convolution fusion | flops 1768161280 | bytes 16547844 | tf_op jit(solution)/shard_map/dot_general | solution.py:29
  246.6 8.3 %add_convert_fusion = bf16[2048,640]{1,0:T(8,128)(2,1)S(1)} fusion(f32[2048,640]{1,0:T(8,128)} %get-tuple-element.932, f32[2048,640]{1,0:T(8,128)} %get-tuple-element.983, bf16[2048,640]{1,0:T(8,128)(2,1)} %all-gather.11.cloned.1.call-done, bf16[2,640,640]{2,1,0:T(8,128)(2,1)S(1)} %copy-done.73), kind=kOutput, calls=%fused_computation.81 | convolution fusion | flops 1696071680 | bytes 16547840 | tf_op jit(solution)/shard_map/dot_general | solution.py:29
  256.5 3.8 convolution_convert_fusion
  260.4 5.7 convolution_convert_fusion.3
  266.2 6.1 %convolution_convert_fusion.2 = bf16[2048,640]{1,0:T(8,128)(2,1)} fusion(bf16[2048,640]{1,0:T(8,128)(2,1)} %get-tuple-element.931, bf16[2,640,640]{2,1,0:T(8,128)(2,1)} %all-gather.7.cloned.1.call-done), kind=kOutput, calls=%fused_computation.115 | convolution fusion | flops 1679032320 | bytes 6062080 | tf_op jit(solution)/shard_map/dot_general | solution.py:39
  272.9 4.2 convolution_bitcast_fusion.2
  277.1 2.4 convolution_bitcast_fusion
  279.5 4.6 convolution_bitcast_fusion.3
  284.1 4.1 convolution_bitcast_fusion.1
  291.3 6.4 %reduce-scatter.15.cloned.1.call-done = bf16[256,640]{1,0:T(8,128)(2,1)} async-done(((bf16[2048,640]{1,0:T(8,128)(2,1)}), bf16[256,640]{1,0:T(8,128)(2,1)}) %reduce-scatter.15.cloned.1.call-update) | async-done | bytes 327696 | tf_op jit(solution)/shard_map/reduce_scatter | solution.py:223
  297.8 1.6 fusion.53
  300.8 35.8 %reduce-scatter.9.cloned.1.call-done = bf16[256,640]{1,0:T(8,128)(2,1)} async-done(((bf16[2048,640]{1,0:T(8,128)(2,1)}), bf16[256,640]{1,0:T(8,128)(2,1)}) %reduce-scatter.9.cloned.1.call-update) | async-done | bytes 327696 | tf_op jit(solution)/shard_map/reduce_scatter | solution.py:214
  336.6 38.8 %reduce-scatter.11.cloned.1.call-done = bf16[256,640]{1,0:T(8,128)(2,1)} async-done(((bf16[2048,640]{1,0:T(8,128)(2,1)}), bf16[256,640]{1,0:T(8,128)(2,1)}) %reduce-scatter.11.cloned.1.call-update) | async-done | bytes 327696 | tf_op jit(solution)/shard_map/reduce_scatter | solution.py:214
  375.4 3.2 bitcast_add_fusion.1
  378.6 1.6 convolution_convert_fusion.7
  380.3 18.7 %while.74 = (s32[]{:T(128)}, bf16[256,1920]{0,1:T(8,128)(2,1)S(1)}, bf16[256,1920]{0,1:T(8,128)(2,1)}, f32[20,256]{1,0:T(8,128)}, f32[20,256]{1,0:T(8,128)}, /*i...) while((s32[]{:T(128)}, bf16[256,1920]{0,1:T(8,128)(2,1)S(1)}, ...), condition=%wide.region_23.25_spmd.clone, body=%wide.region_21.24_spmd.clone.sunk | while | flops 86703120 | bytes 9733514 | solution.py:146
  398.9 2.7 convolution_convert_fusion.6
  402.6 31.9 %while.75 = (s32[]{:T(128)}, bf16[256,1920]{0,1:T(8,128)(2,1)}, bf16[256,1920]{0,1:T(8,128)(2,1)}, f32[20,256]{1,0:T(8,128)}, f32[20,256]{1,0:T(8,128)}, /*index...) while((s32[]{:T(128)}, bf16[256,1920]{0,1:T(8,128)(2,1)}, ...), condition=%wide.region_31.33_spmd.clone, body=%wide.region_29.32_spmd.clone.sunk | while | flops 86703120 | bytes 9733514 | solution.py:146
  435.9 2.2 fusion.63
  439.2 3.3 maximum_add_fusion
  442.6 8.2 %copy.93 = f32[640,2560]{0,1:T(8,128)} copy(f32[640,2560]{1,0:T(8,128)} %maximum_add_fusion) | data formatting | bytes 13107200
  450.8 1.9 copy.72
  452.7 1.8 copy.71
  454.5 1.8 copy.73
  456.3 2.9 fusion.89
  460.2 2.3 fusion.41
  462.5 2.1 multiply_reduce_fusion.3
  464.6 38.9 %all-reduce.1 = f32[2560]{0:T(1024)S(1)} all-reduce(f32[2560]{0:T(1024)S(1)} %maximum_add_fusion.2), channel_id=7, replica_groups=mesh['row'=4,'col'=8] {'row','col'}, use_global_device_ids=true, to_apply=%region_43.45.clone | all-reduce | flops 2560 | bytes 20480
  503.5 2.2 pad_maximum_fusion
  505.9 1.9 fusion.92
  510.3 88.1 %reduce-scatter.19.cloned.1.call-done = f32[80,640]{1,0:T(8,128)} async-done(((f32[2560,640]{1,0:T(8,128)}), f32[80,640]{1,0:T(8,128)}) %reduce-scatter.19.cloned.1.call-update) | async-done | bytes 204816
  (475 shorter events, 100.3 us)
Async XLA Ops:
  7.2 9.0 %copy-start = (f32[2,256,640]{2,1,0:T(8,128)S(1)}, f32[2,256,640]{2,1,0:T(8,128)}, u32[]{:S(2)}) copy-start(f32[2,256,640]{2,1,0:T(8,128)} %param.22) | copy-start | bytes 3932164
  7.2 66.5 %all-gather.5.cloned.1.call-start = ((), (), s32[]{:S(2)}) async-start(), calls=%async_computation.6 | async-start | bytes 3379200 | tf_op jit(solution)/shard_map/all_gather | solution.py:171
  9.0 184.2 %all-gather.7.cloned.1.call-start = ((), (), s32[]{:S(2)}) async-start(), calls=%async_computation.7 | async-start | bytes 2048000 | tf_op jit(solution)/shard_map/all_gather | solution.py:181
  11.0 199.3 %all-gather.9.cloned.1.call-start = ((), (), s32[]{:S(2)}) async-start(), calls=%async_computation.10 | async-start | bytes 2949120 | tf_op jit(solution)/shard_map/all_gather | solution.py:220
  13.3 233.3 %all-gather.11.cloned.1.call-start = ((), (), s32[]{:S(2)}) async-start(), calls=%async_computation.12 | async-start | bytes 2949120 | tf_op jit(solution)/shard_map/all_gather | solution.py:220
  16.2 57.5 %copy-start.47 = (f32[256]{0:T(256)}, f32[256]{0:T(256)S(1)}, u32[]{:S(2)}) copy-start(f32[256]{0:T(256)S(1)} %get-tuple-element.985) | copy-start | bytes 3076
  16.2 66.2 %copy-start.49 = (f32[256]{0:T(256)}, f32[256]{0:T(256)S(1)}, u32[]{:S(2)}) copy-start(f32[256]{0:T(256)S(1)} %get-tuple-element.986) | copy-start | bytes 3076
  16.5 65.9 %copy-start.51 = (f32[256]{0:T(256)}, f32[256]{0:T(256)S(1)}, u32[]{:S(2)}) copy-start(f32[256]{0:T(256)S(1)} %fusion.79) | copy-start | bytes 3076
  16.6 57.1 %copy-start.53 = (f32[256]{0:T(256)}, f32[256]{0:T(256)S(1)}, u32[]{:S(2)}) copy-start(f32[256]{0:T(256)S(1)} %fusion.81) | copy-start | bytes 3076
  59.5 22.9 %copy-start.27 = (f32[640]{0:T(1024)}, f32[640]{0:T(1024)S(1)}, u32[]{:S(2)}) copy-start(f32[640]{0:T(1024)S(1)} %get-tuple-element.974) | copy-start | bytes 7684
  59.5 22.9 %copy-start.29 = (f32[640]{0:T(1024)}, f32[640]{0:T(1024)S(1)}, u32[]{:S(2)}) copy-start(f32[640]{0:T(1024)S(1)} %get-tuple-element.975) | copy-start | bytes 7684
  59.6 44.0 %copy-start.35 = (f32[640]{0:T(1024)}, f32[640]{0:T(1024)S(1)}, u32[]{:S(2)}) copy-start(f32[640]{0:T(1024)S(1)} %get-tuple-element.972) | copy-start | bytes 7684
  84.4 6.4 %copy-start.6 = (bf16[256,1920]{0,1:T(8,128)(2,1)}, bf16[256,1920]{0,1:T(8,128)(2,1)S(1)}, u32[]{:S(2)}) copy-start(bf16[256,1920]{0,1:T(8,128)(2,1)S(1)} %get-tuple-element.1413) | copy-start | bytes 2949124
  84.4 6.4 %copy-start.23 = (s32[256]{0:T(256)}, s32[256]{0:T(256)S(1)}, u32[]{:S(2)}) copy-start(s32[256]{0:T(256)S(1)} %get-tuple-element.1436) | copy-start | bytes 3076
  99.0 87.4 %copy-start.7 = (bf16[256,1920]{0,1:T(8,128)(2,1)}, bf16[256,1920]{0,1:T(8,128)(2,1)S(1)}, u32[]{:S(2)}) copy-start(bf16[256,1920]{0,1:T(8,128)(2,1)S(1)} %get-tuple-element.1414) | copy-start | bytes 2949124
  99.0 87.4 %copy-start.25 = (s32[256]{0:T(256)}, s32[256]{0:T(256)S(1)}, u32[]{:S(2)}) copy-start(s32[256]{0:T(256)S(1)} %get-tuple-element.1437) | copy-start | bytes 3076
  99.0 87.4 %copy-start.39 = (f32[20,256]{1,0:T(8,128)}, f32[20,256]{1,0:T(8,128)S(1)}, u32[]{:S(2)}) copy-start(f32[20,256]{1,0:T(8,128)S(1)} %get-tuple-element.1354) | copy-start | bytes 61444
  99.0 87.4 %copy-start.40 = (f32[20,256]{1,0:T(8,128)}, f32[20,256]{1,0:T(8,128)S(1)}, u32[]{:S(2)}) copy-start(f32[20,256]{1,0:T(8,128)S(1)} %get-tuple-element.1353) | copy-start | bytes 61444
  101.2 91.2 %copy-start.43 = (f32[256]{0:T(256)}, f32[256]{0:T(256)S(1)}, u32[]{:S(2)}) copy-start(f32[256]{0:T(256)S(1)} %broadcast_multiply_fusion) | copy-start | bytes 3076
  101.5 19.9 %copy-start.63 = (f32[256]{0:T(256)}, f32[256]{0:T(256)S(1)}, u32[]{:S(2)}) copy-start(f32[256]{0:T(256)S(1)} %multiply_reduce_fusion.6) | copy-start | bytes 3076
  103.3 106.9 %copy-start.45 = (f32[256]{0:T(256)}, f32[256]{0:T(256)S(1)}, u32[]{:S(2)}) copy-start(f32[256]{0:T(256)S(1)} %broadcast_multiply_fusion.2) | copy-start | bytes 3076
  104.1 8.3 %collective-permute-start = (bf16[256,640]{1,0:T(8,128)(2,1)S(1)}, bf16[256,640]{1,0:T(8,128)(2,1)S(1)}, u32[]{:S(2)}, u32[]{:S(2)}) collective-permute-start(bf16[256,640]{1,0:T(8,128)(2,1)S(1)} %get-tuple-element.970), channel_id=1, source_target_pairs={{0,1},{1,2},{2,3},{3,4},{4,5},{5,6},{6,7},{7,0},{8,9},{9,10},{10,1... | collective-permute-start | bytes 983048 | tf_op jit(solution)/shard_map/ppermute | solution.py:205
  104.4 11.5 %collective-permute-start.7 = (bf16[256,640]{1,0:T(8,128)(2,1)S(1)}, bf16[256,640]{1,0:T(8,128)(2,1)S(1)}, u32[]{:S(2)}, u32[]{:S(2)}) collective-permute-start(bf16[256,640]{1,0:T(8,128)(2,1)S(1)} %get-tuple-element.971), channel_id=1, source_target_pairs={{0,1},{1,2},{2,3},{3,4},{4,5},{5,6},{6,7},{7,0},{8,9},{9,10},{10,1... | collective-permute-start | bytes 983048 | tf_op jit(solution)/shard_map/ppermute | solution.py:205
  112.4 8.9 %collective-permute-start.1 = (bf16[256,640]{1,0:T(8,128)(2,1)S(1)}, bf16[256,640]{1,0:T(8,128)(2,1)S(1)}, u32[]{:S(2)}, u32[]{:S(2)}) collective-permute-start(bf16[256,640]{1,0:T(8,128)(2,1)S(1)} %collective-permute-done), channel_id=1, source_target_pairs={{0,1},{1,2},{2,3},{3,4},{4,5},{5,6},{6,7},{7,0},{8,9},{9,10},{10,1... | collective-permute-start | bytes 983048 | tf_op jit(solution)/shard_map/ppermute | solution.py:205
  116.0 15.9 %collective-permute-start.8 = (bf16[256,640]{1,0:T(8,128)(2,1)S(1)}, bf16[256,640]{1,0:T(8,128)(2,1)S(1)}, u32[]{:S(2)}, u32[]{:S(2)}) collective-permute-start(bf16[256,640]{1,0:T(8,128)(2,1)S(1)} %collective-permute-done.7), channel_id=1, source_target_pairs={{0,1},{1,2},{2,3},{3,4},{4,5},{5,6},{6,7},{7,0},{8,9},{9,10},{10,1... | collective-permute-start | bytes 983048 | tf_op jit(solution)/shard_map/ppermute | solution.py:205
  121.4 21.0 %copy-start.31 = (bf16[256,640]{1,0:T(8,128)(2,1)}, bf16[256,640]{1,0:T(8,128)(2,1)S(1)}, u32[]{:S(2)}) copy-start(bf16[256,640]{1,0:T(8,128)(2,1)S(1)} %collective-permute-done.1) | copy-start | bytes 983044
  121.4 21.0 %collective-permute-start.2 = (bf16[256,640]{1,0:T(8,128)(2,1)S(1)}, bf16[256,640]{1,0:T(8,128)(2,1)S(1)}, u32[]{:S(2)}, u32[]{:S(2)}) collective-permute-start(bf16[256,640]{1,0:T(8,128)(2,1)S(1)} %collective-permute-done.1), channel_id=1, source_target_pairs={{0,1},{1,2},{2,3},{3,4},{4,5},{5,6},{6,7},{7,0},{8,9},{9,10},{10,1... | collective-permute-start | bytes 983048 | tf_op jit(solution)/shard_map/ppermute | solution.py:205
  131.9 20.6 %collective-permute-start.9 = (bf16[256,640]{1,0:T(8,128)(2,1)S(1)}, bf16[256,640]{1,0:T(8,128)(2,1)S(1)}, u32[]{:S(2)}, u32[]{:S(2)}) collective-permute-start(bf16[256,640]{1,0:T(8,128)(2,1)S(1)} %collective-permute-done.8), channel_id=1, source_target_pairs={{0,1},{1,2},{2,3},{3,4},{4,5},{5,6},{6,7},{7,0},{8,9},{9,10},{10,1... | collective-permute-start | bytes 983048 | tf_op jit(solution)/shard_map/ppermute | solution.py:205
  142.4 26.7 %copy-start.32 = (bf16[256,640]{1,0:T(8,128)(2,1)}, bf16[256,640]{1,0:T(8,128)(2,1)S(1)}, u32[]{:S(2)}) copy-start(bf16[256,640]{1,0:T(8,128)(2,1)S(1)} %collective-permute-done.2) | copy-start | bytes 983044
  142.4 13.5 %collective-permute-start.3 = (bf16[256,640]{1,0:T(8,128)(2,1)S(1)}, bf16[256,640]{1,0:T(8,128)(2,1)S(1)}, u32[]{:S(2)}, u32[]{:S(2)}) collective-permute-start(bf16[256,640]{1,0:T(8,128)(2,1)S(1)} %collective-permute-done.2), channel_id=1, source_target_pairs={{0,1},{1,2},{2,3},{3,4},{4,5},{5,6},{6,7},{7,0},{8,9},{9,10},{10,1... | collective-permute-start | bytes 983048 | tf_op jit(solution)/shard_map/ppermute | solution.py:205
  152.4 8.3 %collective-permute-start.10 = (bf16[256,640]{1,0:T(8,128)(2,1)S(1)}, bf16[256,640]{1,0:T(8,128)(2,1)S(1)}, u32[]{:S(2)}, u32[]{:S(2)}) collective-permute-start(bf16[256,640]{1,0:T(8,128)(2,1)S(1)} %collective-permute-done.9), channel_id=1, source_target_pairs={{0,1},{1,2},{2,3},{3,4},{4,5},{5,6},{6,7},{7,0},{8,9},{9,10},{10,1... | collective-permute-start | bytes 983048 | tf_op jit(solution)/shard_map/ppermute | solution.py:205
  155.9 13.2 %copy-start.33 = (bf16[256,640]{1,0:T(8,128)(2,1)}, bf16[256,640]{1,0:T(8,128)(2,1)S(1)}, u32[]{:S(2)}) copy-start(bf16[256,640]{1,0:T(8,128)(2,1)S(1)} %collective-permute-done.3) | copy-start | bytes 983044
  155.9 8.3 %collective-permute-start.4 = (bf16[256,640]{1,0:T(8,128)(2,1)S(1)}, bf16[256,640]{1,0:T(8,128)(2,1)S(1)}, u32[]{:S(2)}, u32[]{:S(2)}) collective-permute-start(bf16[256,640]{1,0:T(8,128)(2,1)S(1)} %collective-permute-done.3), channel_id=1, source_target_pairs={{0,1},{1,2},{2,3},{3,4},{4,5},{5,6},{6,7},{7,0},{8,9},{9,10},{10,1... | collective-permute-start | bytes 983048 | tf_op jit(solution)/shard_map/ppermute | solution.py:205
  160.7 8.4 %collective-permute-start.11 = (bf16[256,640]{1,0:T(8,128)(2,1)S(1)}, bf16[256,640]{1,0:T(8,128)(2,1)}, u32[]{:S(2)}, u32[]{:S(2)}) collective-permute-start(bf16[256,640]{1,0:T(8,128)(2,1)S(1)} %collective-permute-done.10), channel_id=1, source_target_pairs={{0,1},{1,2},{2,3},{3,4},{4,5},{5,6},{6,7},{7,0},{8,9},{9,10},{10,1... | collective-permute-start | bytes 983048 | tf_op jit(solution)/shard_map/ppermute | solution.py:205
  164.2 8.4 %copy-start.34 = (bf16[256,640]{1,0:T(8,128)(2,1)}, bf16[256,640]{1,0:T(8,128)(2,1)S(1)}, u32[]{:S(2)}) copy-start(bf16[256,640]{1,0:T(8,128)(2,1)S(1)} %collective-permute-done.4) | copy-start | bytes 983044
  164.2 8.4 %collective-permute-start.5 = (bf16[256,640]{1,0:T(8,128)(2,1)S(1)}, bf16[256,640]{1,0:T(8,128)(2,1)}, u32[]{:S(2)}, u32[]{:S(2)}) collective-permute-start(bf16[256,640]{1,0:T(8,128)(2,1)S(1)} %collective-permute-done.4), channel_id=1, source_target_pairs={{0,1},{1,2},{2,3},{3,4},{4,5},{5,6},{6,7},{7,0},{8,9},{9,10},{10,1... | collective-permute-start | bytes 983048 | tf_op jit(solution)/shard_map/ppermute | solution.py:205
  169.1 8.6 %collective-permute-start.12 = (bf16[256,640]{1,0:T(8,128)(2,1)}, bf16[256,640]{1,0:T(8,128)(2,1)}, u32[]{:S(2)}, u32[]{:S(2)}) collective-permute-start(bf16[256,640]{1,0:T(8,128)(2,1)} %collective-permute-done.11), channel_id=1, source_target_pairs={{0,1},{1,2},{2,3},{3,4},{4,5},{5,6},{6,7},{7,0},{8,9},{9,10},{10,1... | collective-permute-start | bytes 983048 | tf_op jit(solution)/shard_map/ppermute | solution.py:205
  172.7 8.6 %collective-permute-start.6 = (bf16[256,640]{1,0:T(8,128)(2,1)}, bf16[256,640]{1,0:T(8,128)(2,1)}, u32[]{:S(2)}, u32[]{:S(2)}) collective-permute-start(bf16[256,640]{1,0:T(8,128)(2,1)} %collective-permute-done.5), channel_id=1, source_target_pairs={{0,1},{1,2},{2,3},{3,4},{4,5},{5,6},{6,7},{7,0},{8,9},{9,10},{10,1... | collective-permute-start | bytes 983048 | tf_op jit(solution)/shard_map/ppermute | solution.py:205
  172.7 117.4 %reduce-scatter.13.cloned.1.call-start = ((), (), s32[]{:S(2)}) async-start(), calls=%async_computation.11 | async-start | bytes 2949120 | tf_op jit(solution)/shard_map/reduce_scatter | solution.py:223
  177.8 46.7 %collective-permute-start.13 = (bf16[256,640]{1,0:T(8,128)(2,1)}, bf16[256,640]{1,0:T(8,128)(2,1)}, u32[]{:S(2)}, u32[]{:S(2)}) collective-permute-start(bf16[256,640]{1,0:T(8,128)(2,1)} %collective-permute-done.12), channel_id=1, source_target_pairs={{0,1},{1,2},{2,3},{3,4},{4,5},{5,6},{6,7},{7,0},{8,9},{9,10},{10,1... | collective-permute-start | bytes 983048 | tf_op jit(solution)/shard_map/ppermute | solution.py:205
  210.2 10.2 %copy-start.72 = (bf16[2,640,640]{2,1,0:T(8,128)(2,1)S(1)}, bf16[2,640,640]{2,1,0:T(8,128)(2,1)}, u32[]{:S(2)}) copy-start(bf16[2,640,640]{2,1,0:T(8,128)(2,1)} %all-gather.7.cloned.1.call-done) | copy-start | bytes 4915204
  224.2 73.6 %reduce-scatter.15.cloned.1.call-start = ((), (), s32[]{:S(2)}) async-start(), calls=%async_computation.13 | async-start | bytes 2949120 | tf_op jit(solution)/shard_map/reduce_scatter | solution.py:223
  229.3 17.3 %copy-start.73 = (bf16[2,640,640]{2,1,0:T(8,128)(2,1)S(1)}, bf16[2,640,640]{2,1,0:T(8,128)(2,1)}, u32[]{:S(2)}) copy-start(bf16[2,640,640]{2,1,0:T(8,128)(2,1)} %all-gather.7.cloned.1.call-done) | copy-start | bytes 4915204
  260.3 76.2 %reduce-scatter.9.cloned.1.call-start = ((), (), s32[]{:S(2)}) async-start(), calls=%async_computation.8 | async-start | bytes 2949120 | tf_op jit(solution)/shard_map/reduce_scatter | solution.py:214
  266.1 109.3 %reduce-scatter.11.cloned.1.call-start = ((), (), s32[]{:S(2)}) async-start(), calls=%async_computation.9 | async-start | bytes 2949120 | tf_op jit(solution)/shard_map/reduce_scatter | solution.py:214
  266.2 6.7 %copy-start.70 = (bf16[2048,640]{1,0:T(8,128)(2,1)S(1)}, bf16[2048,640]{1,0:T(8,128)(2,1)}, u32[]{:S(2)}) copy-start(bf16[2048,640]{1,0:T(8,128)(2,1)} %all-gather.9.cloned.1.call-done) | copy-start | bytes 7864324
  272.3 184.0 %reduce-scatter.17.cloned.1.call-start = ((), (), s32[]{:S(2)}) async-start(), calls=%async_computation.14 | async-start | bytes 2048000 | tf_op jit(solution)/shard_map/reduce_scatter | solution.py:249
  288.3 9.5 %copy-start.3 = (f32[256,640]{1,0:T(8,128)S(1)}, f32[256,640]{1,0:T(8,128)}, u32[]{:S(2)}) copy-start(f32[256,640]{1,0:T(8,128)} %copy-done.2) | copy-start | bytes 1966084
  288.3 9.5 %copy-start.44 = (f32[256]{0:T(256)S(1)}, f32[256]{0:T(256)}, u32[]{:S(2)}) copy-start(f32[256]{0:T(256)} %copy-done.43) | copy-start | bytes 3076
  288.3 9.5 %copy-start.56 = (f32[256]{0:T(256)S(1)}, f32[256]{0:T(256)}, u32[]{:S(2)}) copy-start(f32[256]{0:T(256)} %copy-done.55) | copy-start | bytes 3076
  288.3 11.1 %copy-start.64 = (f32[256]{0:T(256)S(1)}, f32[256]{0:T(256)}, u32[]{:S(2)}) copy-start(f32[256]{0:T(256)} %copy-done.63) | copy-start | bytes 3076
  288.3 11.1 %copy-start.58 = (f32[256]{0:T(256)S(1)}, f32[256]{0:T(256)}, u32[]{:S(2)}) copy-start(f32[256]{0:T(256)} %copy-done.57) | copy-start | bytes 3076
  289.8 308.6 %reduce-scatter.19.cloned.1.call-start = ((), (), s32[]{:S(2)}) async-start(), calls=%async_computation.15 | async-start | bytes 6758400
  299.4 80.9 %copy-start.26 = (s32[256]{0:T(256)S(1)}, s32[256]{0:T(256)}, u32[]{:S(2)}) copy-start(s32[256]{0:T(256)} %copy-done.25) | copy-start | bytes 3076
  380.2 22.4 %copy-start.24 = (s32[256]{0:T(256)S(1)}, s32[256]{0:T(256)}, u32[]{:S(2)}) copy-start(s32[256]{0:T(256)} %copy-done.23) | copy-start | bytes 3076
  402.6 31.9 %copy-start.15 = (bf16[256,640]{0,1:T(8,128)(2,1)S(1)}, bf16[256,640]{0,1:T(8,128)(2,1)}, u32[]{:S(2)}) copy-start(bf16[256,640]{0,1:T(8,128)(2,1)} %copy-done.14) | copy-start | bytes 983044
  402.6 32.4 %copy-start.16 = (bf16[256,640]{0,1:T(8,128)(2,1)S(1)}, bf16[256,640]{0,1:T(8,128)(2,1)}, u32[]{:S(2)}) copy-start(bf16[256,640]{0,1:T(8,128)(2,1)} %get-tuple-element.686) | copy-start | bytes 983044
  460.2 43.3 %copy-start.17 = (f32[1,256,640]{2,1,0:T(8,128)S(1)}, f32[1,256,640]{2,1,0:T(8,128)}, u32[]{:S(2)}) copy-start(f32[1,256,640]{2,1,0:T(8,128)} %get-tuple-element.967) | copy-start | bytes 1966084
  462.5 43.2 %copy-start.62 = (f32[256]{0:T(256)S(1)}, f32[256]{0:T(256)}, u32[]{:S(2)}) copy-start(f32[256]{0:T(256)} %copy-done.61) | copy-start | bytes 3076
  462.5 43.2 %copy-start.60 = (f32[256]{0:T(256)S(1)}, f32[256]{0:T(256)}, u32[]{:S(2)}) copy-start(f32[256]{0:T(256)} %copy-done.59) | copy-start | bytes 3076
  505.8 93.7 %copy-start.18 = (f32[640,80]{1,0:T(8,128)S(1)}, f32[640,80]{1,0:T(8,128)}, u32[]{:S(2)}) copy-start(f32[640,80]{1,0:T(8,128)} %copy.72) | copy-start | bytes 614404
  505.8 93.7 %copy-start.19 = (f32[640,80]{1,0:T(8,128)S(1)}, f32[640,80]{1,0:T(8,128)}, u32[]{:S(2)}) copy-start(f32[640,80]{1,0:T(8,128)} %copy.71) | copy-start | bytes 614404
  507.7 92.8 %copy-start.20 = (f32[640,80]{1,0:T(8,128)S(1)}, f32[640,80]{1,0:T(8,128)}, u32[]{:S(2)}) copy-start(f32[640,80]{1,0:T(8,128)} %copy.73) | copy-start | bytes 614404
  509.8 93.2 %copy-start.69 = (f32[80]{0:T(128)}, f32[80]{0:T(128)S(1)}, u32[]{:S(2)}) copy-start(f32[80]{0:T(128)S(1)} %get-tuple-element.920) | copy-start | bytes 964
  (40 other events, 94.6 us)
Sparse Core Ops, SparseCore 0:
  11.5 62.1 all-gather.4
  76.1 30.4 all-gather.6
  108.3 45.7 all-gather.8
  172.8 36.2 all-gather.10
  224.3 34.7 reduce-scatter.12
  261.3 36.4 reduce-scatter.14
  300.1 36.4 reduce-scatter.8
  338.9 36.4 reduce-scatter.10
  378.4 30.4 reduce-scatter.16
  450.9 147.4 reduce-scatter.18
